TPU v7x, 256 devices: a whole 4x4x8 slice. The times are simulated.
256 devices in a mesh: head: 8 (over z), page: 32 (over y, x, core).
Axes of the slice: x: 4, y: 4, z: 8, core: 2. Of those that a mesh axis runs over, the one named last changes fastest.
Arguments:
- doc_states: bfloat16 [2048, 2048], P('page'), may hold values from -6 to 6
- gain_attn: float32 [2048], replicated, may hold values from 0.1 to 1.9
- query_weight: bfloat16 [2048, 2048], P(None, 'head'), may hold values from -0.125 to 0.125
- cache_keys: bfloat16 [64, 128, 2048], P('page', None, 'head'), may hold values from -144 to 144
- cache_values: bfloat16 [64, 128, 2048], P('page', None, 'head'), may hold values from -6 to 6
- rel_bucket: int32 [64, 128], P('page'), may hold values from 0 to 31
- bias_table: float32 [32, 32], P(None, 'head'), may hold values from -4 to 4
- out_weight: bfloat16 [2048, 2048], P('head'), may hold values from -0.125 to 0.125
- gain_ffn: float32 [2048], replicated, may hold values from 0.1 to 1.9
- wi_gate: bfloat16 [2048, 5120], P(None, 'head'), may hold values from -0.125 to 0.125
- wi_up: bfloat16 [2048, 5120], P(None, 'head'), may hold values from -0.125 to 0.125
- wo_ffn: bfloat16 [5120, 2048], P('head'), may hold values from -0.078125 to 0.078125
- score_vector: float32 [2048], replicated, may hold values from -0.125 to 0.125
- query_lengths: int32 [8], replicated, may hold values from 1 to 1024
- doc_query: int32 [256], replicated, may hold values from 0 to 7
- doc_of_token: int32 [2048], replicated, may hold values from 0 to 255, as said below
- page_table: int32 [64], replicated, may hold values from 0 to 63, each once
Outputs:
- doc_scores: float32 [256], P('page')
Inputs may be any that keep to these rules, and one draw needn't show every extreme that they name: page_table lists every physical page once. `doc_of_token`: the tokens of each document form one contiguous run of 1 to 256 tokens; every document has one run, and some document has exactly 256 tokens.
All inputs are finite; a program needn't handle non-finite values.
Results may differ from a plain program's by a relative error of at most 0.03.
Values may be sent and summed in bfloat16 or wider, within the bound.
No kernel may reach another device: no remote copies, remote signals or barrier semaphores. Data moves between devices by JAX's collectives and lax.ppermute only.
A program may use at most 320 MiB of HBM per device.

v0:
```python
import jax
import jax.numpy as jnp
from jax import lax
from jax.sharding import PartitionSpec as P

NQ = 8


def combined_all(value, axis, join):
    pieces = jax.tree.map(lambda part: lax.all_gather(part, axis), value)
    head = jax.tree.map(lambda part: part[0], pieces)
    tail = jax.tree.map(lambda part: part[1:], pieces)
    so_far, _ = lax.scan(lambda so_far, section: (join(so_far, section), None), head, tail)
    return so_far


def rms_scale(values, gain):
    values = values.astype(jnp.float32)
    return values * lax.rsqrt(jnp.mean(values * values, axis=-1, keepdims=True) + 1e-06) * gain


def combine_parts(first, second):
    top_a, total_a, sums_a = first
    top_b, total_b, sums_b = second
    top = jnp.maximum(top_a, top_b)
    scale_a = jnp.exp(top_a - top)
    scale_b = jnp.exp(top_b - top)
    depth = sums_a.shape[1] // top.shape[1]
    sums = sums_a * jnp.repeat(scale_a, depth, axis=1) + sums_b * jnp.repeat(scale_b, depth, axis=1)
    return (top, total_a * scale_a + total_b * scale_b, sums)


def per_device(
    doc_states,
    gain_attn,
    query_weight,
    cache_keys,
    cache_values,
    rel_bucket,
    bias_table,
    out_weight,
    gain_ffn,
    wi_gate,
    wi_up,
    wo_ffn,
    score_vector,
    query_lengths,
    doc_query,
    doc_of_token,
    page_table,
):
    tok_dev = doc_states.shape[0]
    local_pages, page_len, local_width = cache_keys.shape
    local_heads = bias_table.shape[1]
    depth = local_width // local_heads
    key_count = local_pages * page_len
    all_pages = page_table.shape[0]
    max_pages = all_pages // NQ
    page_rank = lax.axis_index("page")
    normed = rms_scale(doc_states, gain_attn).astype(jnp.bfloat16)
    queries = jnp.dot(normed, query_weight, preferred_element_type=jnp.float32).astype(jnp.bfloat16)
    gathered = lax.all_gather(queries, "page", axis=0, tiled=True)
    total_rows = gathered.shape[0]
    doc_ids = jnp.arange(doc_query.shape[0], dtype=jnp.int32)
    tok_query = jnp.sum(
        jnp.where(doc_of_token[:, None] == doc_ids[None, :], doc_query[None, :], 0), axis=1
    )
    page_ids = page_rank * local_pages + jnp.arange(local_pages, dtype=jnp.int32)
    slots = jnp.arange(all_pages, dtype=jnp.int32)
    located = jnp.sum(
        jnp.where(page_table[None, :] == page_ids[:, None], slots[None, :], 0), axis=1
    )
    owner = located // max_pages
    logical = located % max_pages
    query_ids = jnp.arange(NQ, dtype=jnp.int32)
    owner_len = jnp.sum(
        jnp.where(owner[:, None] == query_ids[None, :], query_lengths[None, :], 0), axis=1
    )
    position = logical[:, None] * page_len + jnp.arange(page_len, dtype=jnp.int32)[None, :]
    key_query = jnp.where(position < owner_len[:, None], owner[:, None], -1).reshape(key_count)
    buckets = jnp.arange(bias_table.shape[0], dtype=jnp.int32)
    onehot = (rel_bucket.reshape(key_count)[None, :] == buckets[:, None]).astype(jnp.float32)
    key_bias = jnp.dot(bias_table.T, onehot, precision=lax.Precision.HIGHEST)
    keys = cache_keys.reshape(key_count, local_heads, depth)
    values = cache_values.reshape(key_count, local_heads, depth)
    block = min(512, total_rows)
    count = total_rows // block

    def partial_block(pair):
        rows, owners = pair
        heads = rows.reshape(block, local_heads, depth)
        scores = (
            jnp.einsum("rhd,khd->rhk", heads, keys, preferred_element_type=jnp.float32)
            + key_bias[None]
        )
        mask = (owners[:, None] == key_query[None, :])[:, None, :]
        top = jnp.max(jnp.where(mask, scores, -1e30), axis=-1)
        weights = jnp.where(mask, jnp.exp(scores - top[..., None]), 0.0)
        total = jnp.sum(weights, axis=-1)
        summed = jnp.einsum(
            "rhk,khd->rhd", weights.astype(jnp.bfloat16), values, preferred_element_type=jnp.float32
        )
        return (top, total, summed.reshape(block, local_width))

    tops, totals, summed = lax.map(
        partial_block,
        (gathered.reshape(count, block, local_width), tok_query.reshape(count, block)),
    )
    tops = tops.reshape(total_rows, local_heads)
    totals = totals.reshape(total_rows, local_heads)
    summed = summed.reshape(total_rows, local_width)
    row_start = page_rank * tok_dev
    joined_top, joined_total, joined_sums = combined_all(
        (tops, totals, summed), "page", combine_parts
    )
    own_total = lax.dynamic_slice_in_dim(joined_total, row_start, tok_dev, 0)
    own_sums = lax.dynamic_slice_in_dim(joined_sums, row_start, tok_dev, 0)
    context = (own_sums / jnp.repeat(own_total, depth, axis=1)).astype(jnp.bfloat16)
    projected = lax.psum(
        jnp.dot(context, out_weight, preferred_element_type=jnp.float32).astype(jnp.bfloat16),
        "head",
    ).astype(jnp.float32)
    hidden = doc_states.astype(jnp.float32) + projected
    normed_two = rms_scale(hidden, gain_ffn).astype(jnp.bfloat16)
    gate = jnp.dot(normed_two, wi_gate, preferred_element_type=jnp.float32)
    upper = jnp.dot(normed_two, wi_up, preferred_element_type=jnp.float32)
    middle = (jax.nn.gelu(gate, approximate=True) * upper).astype(jnp.bfloat16)
    ffn_part = jnp.dot(middle, wo_ffn, preferred_element_type=jnp.float32)
    final = hidden + lax.psum(ffn_part.astype(jnp.bfloat16), "head").astype(jnp.float32)
    tok_score = jnp.dot(final, score_vector, precision=lax.Precision.HIGHEST)
    own_docs = lax.dynamic_slice_in_dim(doc_of_token, row_start, tok_dev, 0)
    member = (own_docs[:, None] == doc_ids[None, :]).astype(jnp.float32)
    doc_sums = jnp.dot(tok_score, member, precision=lax.Precision.HIGHEST)
    pooled = lax.psum_scatter(doc_sums, "page", scatter_dimension=0, tiled=True)
    doc_dev = pooled.shape[0]
    mine = page_rank * doc_dev + jnp.arange(doc_dev, dtype=jnp.int32)
    counts = jnp.sum((doc_of_token[:, None] == mine[None, :]).astype(jnp.float32), axis=0)
    return pooled / counts


def solution(mesh):
    return jax.shard_map(
        per_device,
        mesh=mesh,
        in_specs=(
            P("page", None),
            P(),
            P(None, "head"),
            P("page", None, "head"),
            P("page", None, "head"),
            P("page", None),
            P(None, "head"),
            P("head", None),
            P(),
            P(None, "head"),
            P(None, "head"),
            P("head", None),
            P(),
            P(),
            P(),
            P(),
            P(),
        ),
        out_specs=P("page"),
        check_vma=False,
    )
```

profile of v0, /device:TPU:1, one launch (start us, length us, event | category | flops | bytes accessed | tf_op | source)
XLA Modules:
  0.0 1019.1 jit_solution(12967437557516146246)
XLA Ops:
  14.0 48.3 %all-gather.5.cloned.1.call-done = bf16[2048,256]{1,0:T(8,128)(2,1)} async-done(((bf16[64,256]{1,0:T(8,128)(2,1)}), bf16[2048,256]{1,0:T(8,128)(2,1)}) %all-gather.5.cloned.1.call-update) | async-done | bytes 1048592 | tf_op jit(solution)/shard_map/all_gather | solution.py:62
  62.4 41.0 %while.30 = (s32[]{:T(128)}, f32[4,512,4]{1,2,0:T(4,128)}, f32[4,512,4]{1,2,0:T(4,128)}, f32[4,512,256]{2,1,0:T(8,128)}, s32[4,512]{1,0:T(4,128)S(1)}, /*index=5...) while((s32[]{:T(128)}, f32[4,512,4]{1,2,0:T(4,128)}, ...), condition=%wide.region_7.8_spmd.clone, body=%wide.region_4.7_spmd.clone.sunk | while | flops 140112640 | bytes 19551472 | solution.py:105
  104.7 46.0 %all-gather.7.cloned.1.call-done = f32[32,2048,4]{1,2,0:T(4,128)} async-done(((f32[1,2048,4]{1,2,0:T(4,128)}), f32[32,2048,4]{1,2,0:T(4,128)}) %all-gather.7.cloned.1.call-update) | async-done | bytes 1048592 | tf_op jit(solution)/shard_map/all_gather | solution.py:10
  153.0 47.5 %all-gather.9.cloned.1.call-done = f32[32,2048,4]{1,2,0:T(4,128)} async-done(((f32[1,2048,4]{1,2,0:T(4,128)}), f32[32,2048,4]{1,2,0:T(4,128)}) %all-gather.9.cloned.1.call-update) | async-done | bytes 1048592 | tf_op jit(solution)/shard_map/all_gather | solution.py:10
  204.3 204.0 %all-gather.11.cloned.1.call-done = f32[32,2048,256]{2,1,0:T(8,128)} async-done(((f32[1,2048,256]{2,1,0:T(8,128)}), f32[32,2048,256]{2,1,0:T(8,128)}) %all-gather.11.cloned.1.call-update) | async-done | bytes 67108880 | tf_op jit(solution)/shard_map/all_gather | solution.py:10
  414.3 43.9 %slice.29 = f32[31,2048,256]{2,1,0:T(8,128)} slice(f32[32,2048,256]{2,1,0:T(8,128)} %all-gather.11.cloned.1.call-done), slice={[1:32], [0:2048], [0:256]} | slice | bytes 130023424 | tf_op jit(solution)/shard_map/slice | solution.py:12
  458.2 335.9 %while.29 = (s32[]{:T(128)}, f32[2048,4]{0,1:T(4,128)S(1)}, f32[2048,4]{0,1:T(4,128)S(1)}, f32[2048,256]{0,1:T(8,128)}, f32[31,2048,4]{1,2,0:T(4,128)}, /*index=...) while((s32[]{:T(128)}, f32[2048,4]{0,1:T(4,128)S(1)}, f32[2048,4]{0,1:T(4,128)S(1)}, ...), condition=%wide.region_9.10_spmd, body=%wide.region_8.9_spmd.sunk | while | flops 1622018 | bytes 15007837 | solution.py:13
  465.1 4.0 fusion.75
  486.8 4.0 fusion.75
  497.6 4.0 fusion.75
  508.4 4.0 fusion.75
  519.3 4.0 fusion.75
  530.1 4.0 fusion.75
  540.9 4.0 fusion.75
  551.8 4.0 fusion.75
  562.6 4.0 fusion.75
  573.4 4.0 fusion.75
  584.3 4.0 fusion.75
  605.9 4.0 fusion.75
  627.6 4.0 fusion.75
  649.3 4.0 fusion.75
  797.6 66.7 %all-reduce.4.cloned.1.call-done = bf16[64,2048]{1,0:T(8,128)(2,1)} async-done(((bf16[64,2048]{1,0:T(8,128)(2,1)}), bf16[64,2048]{1,0:T(8,128)(2,1)}) %all-reduce.4.cloned.1.call-update) | async-done | bytes 262160 | tf_op jit(solution)/shard_map/psum | solution.py:119
  873.2 69.5 %all-reduce.6.cloned.1.call-done = bf16[64,2048]{1,0:T(8,128)(2,1)} async-done(((bf16[64,2048]{1,0:T(8,128)(2,1)}), bf16[64,2048]{1,0:T(8,128)(2,1)}) %all-reduce.6.cloned.1.call-update) | async-done | bytes 262160 | tf_op jit(solution)/shard_map/psum | solution.py:129
  944.4 67.2 %all-reduce = f32[256]{0:T(256)S(1)} all-reduce(f32[256]{0:T(256)S(1)} %bitcast.123), channel_id=2, replica_groups=mesh['head'=8,'page'=32] {'page'}, use_global_device_ids=true, to_apply=%region_13.14.clone | all-reduce | flops 256 | bytes 2048
  (255 shorter events, 354.6 us)
Async XLA Ops:
  6.5 861.5 %copy-start = (bf16[640,2048]{1,0:T(8,128)(2,1)S(1)}, bf16[640,2048]{1,0:T(8,128)(2,1)}, u32[]{:S(2)}) copy-start(bf16[640,2048]{1,0:T(8,128)(2,1)} %param.32) | copy-start | bytes 7864324
  6.5 4.9 copy-start.4
  6.5 5.1 copy-start.11
  6.5 5.1 copy-start.8
  6.5 5.9 copy-start.14
  6.5 6.6 copy-start.15
  6.6 7.4 copy-start.13
  6.6 7.3 copy-start.12
  6.6 55.8 %all-gather.5.cloned.1.call-start = ((), (), s32[]{:S(2)}) async-start(), calls=%async_computation | async-start | bytes 1081344 | tf_op jit(solution)/shard_map/all_gather | solution.py:62
  10.2 140.5 %all-gather.7.cloned.1.call-start = ((), (), s32[]{:S(2)}) async-start(), calls=%async_computation.1 | async-start | bytes 1081344 | tf_op jit(solution)/shard_map/all_gather | solution.py:10
  69.9 2.8 copy-start.6
  80.1 2.8 copy-start.6
  90.4 2.8 copy-start.6
  100.6 2.8 copy-start.6
  103.4 97.1 %all-gather.9.cloned.1.call-start = ((), (), s32[]{:S(2)}) async-start(), calls=%async_computation.2 | async-start | bytes 1081344 | tf_op jit(solution)/shard_map/all_gather | solution.py:10
  104.1 304.3 %all-gather.11.cloned.1.call-start = ((), (), s32[]{:S(2)}) async-start(), calls=%async_computation.3 | async-start | bytes 69206016 | tf_op jit(solution)/shard_map/all_gather | solution.py:10
  104.7 759.6 %all-reduce.4.cloned.1.call-start = ((), (), s32[]{:S(2)}) async-start(), calls=%async_computation.4 | async-start | bytes 524288 | tf_op jit(solution)/shard_map/psum | solution.py:119
  458.2 406.1 %copy-start.2 = (bf16[64,2048]{1,0:T(8,128)(2,1)S(1)}, bf16[64,2048]{1,0:T(8,128)(2,1)}, u32[]{:S(2)}) copy-start(bf16[64,2048]{1,0:T(8,128)(2,1)} %param.21) | copy-start | bytes 786436
  794.2 71.4 %copy-start.7 = (f32[2048]{0:T(1024)S(1)}, f32[2048]{0:T(1024)}, u32[]{:S(2)}) copy-start(f32[2048]{0:T(1024)} %param.29) | copy-start | bytes 24580
  797.5 145.2 %all-reduce.6.cloned.1.call-start = ((), (), s32[]{:S(2)}) async-start(), calls=%async_computation.5 | async-start | bytes 524288 | tf_op jit(solution)/shard_map/psum | solution.py:129
  864.3 3.7 copy-start.3
  868.0 3.6 copy-start.9
  868.0 3.7 copy-start.16
  868.0 74.7 %copy-start.10 = (f32[2048]{0:T(1024)S(1)}, f32[2048]{0:T(1024)}, u32[]{:S(2)}) copy-start(f32[2048]{0:T(1024)} %param.33) | copy-start | bytes 24580
  (8 other events, 9.1 us)
Sparse Core Ops, SparseCore 0:
  10.3 52.0 all-gather.4
  103.5 47.1 all-gather.6
  153.3 47.1 all-gather.8
  202.9 205.4 all-gather.10
  797.6 66.6 all-reduce.3
  871.8 70.8 all-reduce.5
where the time goes:
time: 1020 us
  waiting for transfers between devices  483 us (47%)
  local copies, waits for them, and re-layouts  264 us (26%)
  other arithmetic  170 us (17%)
  blocking collectives  67.2 us (7%)
  matrix products  20.4 us (2%)
  between operations  14.4 us (1%)
    all_gather x3, waiting for transfers between devices, combined_all(): pieces = jax.tree.map(lambda part: lax.all_gather(part, axis), value)  298 us
    dynamic_slice x62, local copies, waits for them, and re-layouts, combined_all(): lax.scan(lambda so_far, section: (join(so_far, section), None), head, tail)  185 us
    add x31, other arithmetic, combine_parts(): sums_a * jnp.repeat(scale_a, depth, axis=1)  125 us
    psum x1, waiting for transfers between devices, per_device(): lax.psum(ffn_part.astype(jnp.bfloat16), 'head').astype(jnp.float32)  69.5 us
    unnamed x1, blocking collectives  67.2 us
    psum x1, waiting for transfers between devices, per_device(): lax.psum(jnp.dot(context, out_weight, preferred_element_type=jnp.float32)...  66.7 us
    slice x3, local copies, waits for them, and re-layouts, combined_all(): tail = jax.tree.map(lambda part: part[1:], pieces)  48.5 us
    all_gather x1, waiting for transfers between devices, per_device(): gathered = lax.all_gather(queries, 'page', axis=0, tiled=True)  48.3 us
  transfers between devices with their start and end apart: 6, of which 6 were waited for; matrix products, arithmetic and copies ran while one was open for 1% of the time, Pallas kernels for 0%

commit v1 on v0

--- a/solution.py
+++ b/solution.py
@@ -126,7 +126,9 @@
     upper = jnp.dot(normed_two, wi_up, preferred_element_type=jnp.float32)
     middle = (jax.nn.gelu(gate, approximate=True) * upper).astype(jnp.bfloat16)
     ffn_part = jnp.dot(middle, wo_ffn, preferred_element_type=jnp.float32)
-    final = hidden + lax.psum(ffn_part.astype(jnp.bfloat16), "head").astype(jnp.float32)
+    final = hidden + jnp.sum(lax.all_gather(ffn_part.astype(jnp.bfloat16), "head"), axis=0).astype(
+        jnp.float32
+    )
     tok_score = jnp.dot(final, score_vector, precision=lax.Precision.HIGHEST)
     own_docs = lax.dynamic_slice_in_dim(doc_of_token, row_start, tok_dev, 0)
     member = (own_docs[:, None] == doc_ids[None, :]).astype(jnp.float32)

time: 1020 us -> 994 us (0.975)
  waiting for transfers between devices: 483 us -> 453 us
    psum x1 -> x0, waiting for transfers between devices: 69.5 us -> none  [per_device(): lax.psum(ffn_part.astype(jnp.bfloat16), 'head').astype(jnp.float32)]
    all_gather x0 -> x1, waiting for transfers between devices: none -> 39 us  [per_device(): lax.all_gather(ffn_part.astype(jnp.bfloat16), 'head')]
where the time goes in v1:
time: 994 us; the launch traced here: 989 us
  waiting for transfers between devices  453 us (46%)
  local copies, waits for them, and re-layouts  264 us (27%)
  other arithmetic  172 us (17%)
  blocking collectives  66.4 us (7%)
  matrix products  19.4 us (2%)
  between operations  14.4 us (1%)
    all_gather x3, waiting for transfers between devices, combined_all(): pieces = jax.tree.map(lambda part: lax.all_gather(part, axis), value)  298 us
    dynamic_slice x62, local copies, waits for them, and re-layouts, combined_all(): lax.scan(lambda so_far, section: (join(so_far, section), None), head, tail)  185 us
    add x31, other arithmetic, combine_parts(): sums_a * jnp.repeat(scale_a, depth, axis=1)  125 us
    psum x1, waiting for transfers between devices, per_device(): lax.psum(jnp.dot(context, out_weight, preferred_element_type=jnp.float32)...  66.7 us
    unnamed x1, blocking collectives  66.4 us
    slice x3, local copies, waits for them, and re-layouts, combined_all(): tail = jax.tree.map(lambda part: part[1:], pieces)  48.5 us
    all_gather x1, waiting for transfers between devices, per_device(): gathered = lax.all_gather(queries, 'page', axis=0, tiled=True)  48.3 us
    all_gather x1, waiting for transfers between devices, per_device(): lax.all_gather(ffn_part.astype(jnp.bfloat16), 'head')  39 us
  transfers between devices with their start and end apart: 6, of which 6 were waited for; matrix products, arithmetic and copies ran while one was open for 1% of the time, Pallas kernels for 0%

profile of v1, /device:TPU:1, one launch (start us, length us, event | category | flops | bytes accessed | tf_op | source)
XLA Modules:
  0.0 988.8 jit_solution(12342755481087112973)
XLA Ops:
  14.0 48.3 %all-gather.7.cloned.1.call-done = bf16[2048,256]{1,0:T(8,128)(2,1)} async-done(((bf16[64,256]{1,0:T(8,128)(2,1)}), bf16[2048,256]{1,0:T(8,128)(2,1)}) %all-gather.7.cloned.1.call-update) | async-done | bytes 1048592 | tf_op jit(solution)/shard_map/all_gather | solution.py:62
  62.4 41.0 %while.30 = (s32[]{:T(128)}, f32[4,512,4]{1,2,0:T(4,128)}, f32[4,512,4]{1,2,0:T(4,128)}, f32[4,512,256]{2,1,0:T(8,128)}, s32[4,512]{1,0:T(4,128)S(1)}, /*index=5...) while((s32[]{:T(128)}, f32[4,512,4]{1,2,0:T(4,128)}, ...), condition=%wide.region_7.8_spmd.clone, body=%wide.region_4.7_spmd.clone.sunk | while | flops 140112640 | bytes 19551472 | solution.py:105
  104.7 46.0 %all-gather.9.cloned.1.call-done = f32[32,2048,4]{1,2,0:T(4,128)} async-done(((f32[1,2048,4]{1,2,0:T(4,128)}), f32[32,2048,4]{1,2,0:T(4,128)}) %all-gather.9.cloned.1.call-update) | async-done | bytes 1048592 | tf_op jit(solution)/shard_map/all_gather | solution.py:10
  153.0 47.5 %all-gather.11.cloned.1.call-done = f32[32,2048,4]{1,2,0:T(4,128)} async-done(((f32[1,2048,4]{1,2,0:T(4,128)}), f32[32,2048,4]{1,2,0:T(4,128)}) %all-gather.11.cloned.1.call-update) | async-done | bytes 1048592 | tf_op jit(solution)/shard_map/all_gather | solution.py:10
  204.3 204.0 %all-gather.13.cloned.1.call-done = f32[32,2048,256]{2,1,0:T(8,128)} async-done(((f32[1,2048,256]{2,1,0:T(8,128)}), f32[32,2048,256]{2,1,0:T(8,128)}) %all-gather.13.cloned.1.call-update) | async-done | bytes 67108880 | tf_op jit(solution)/shard_map/all_gather | solution.py:10
  414.3 43.9 %slice.29 = f32[31,2048,256]{2,1,0:T(8,128)} slice(f32[32,2048,256]{2,1,0:T(8,128)} %all-gather.13.cloned.1.call-done), slice={[1:32], [0:2048], [0:256]} | slice | bytes 130023424 | tf_op jit(solution)/shard_map/slice | solution.py:12
  458.2 335.9 %while.29 = (s32[]{:T(128)}, f32[2048,4]{0,1:T(4,128)S(1)}, f32[2048,4]{0,1:T(4,128)S(1)}, f32[2048,256]{0,1:T(8,128)}, f32[31,2048,4]{1,2,0:T(4,128)}, /*index=...) while((s32[]{:T(128)}, f32[2048,4]{0,1:T(4,128)S(1)}, f32[2048,4]{0,1:T(4,128)S(1)}, ...), condition=%wide.region_9.10_spmd, body=%wide.region_8.9_spmd.sunk | while | flops 1622018 | bytes 15007837 | solution.py:13
  465.1 4.0 fusion.75
  486.8 4.0 fusion.75
  497.6 4.0 fusion.75
  508.4 4.0 fusion.75
  519.3 4.0 fusion.75
  530.1 4.0 fusion.75
  540.9 4.0 fusion.75
  551.8 4.0 fusion.75
  562.6 4.0 fusion.75
  573.4 4.0 fusion.75
  584.3 4.0 fusion.75
  605.9 4.0 fusion.75
  627.6 4.0 fusion.75
  649.3 4.0 fusion.75
  797.6 66.7 %all-reduce.3.cloned.1.call-done = bf16[64,2048]{1,0:T(8,128)(2,1)} async-done(((bf16[64,2048]{1,0:T(8,128)(2,1)}), bf16[64,2048]{1,0:T(8,128)(2,1)}) %all-reduce.3.cloned.1.call-update) | async-done | bytes 262160 | tf_op jit(solution)/shard_map/psum | solution.py:119
  873.2 39.0 %all-gather.15.cloned.1.call-done = bf16[512,2048]{1,0:T(8,128)(2,1)} async-done(((bf16[64,2048]{1,0:T(8,128)(2,1)}), bf16[512,2048]{1,0:T(8,128)(2,1)}) %all-gather.15.cloned.1.call-update) | async-done | bytes 2097168 | tf_op jit(solution)/shard_map/all_gather | solution.py:129
  914.9 66.4 %all-reduce = f32[256]{0:T(256)S(1)} all-reduce(f32[256]{0:T(256)S(1)} %bitcast.125), channel_id=3, replica_groups=mesh['head'=8,'page'=32] {'page'}, use_global_device_ids=true, to_apply=%region_13.14.clone | all-reduce | flops 256 | bytes 2048
  (256 shorter events, 355.6 us)
Async XLA Ops:
  6.5 861.5 %copy-start = (bf16[640,2048]{1,0:T(8,128)(2,1)S(1)}, bf16[640,2048]{1,0:T(8,128)(2,1)}, u32[]{:S(2)}) copy-start(bf16[640,2048]{1,0:T(8,128)(2,1)} %param.32) | copy-start | bytes 7864324
  6.5 4.9 copy-start.4
  6.5 5.1 copy-start.11
  6.5 5.1 copy-start.8
  6.5 5.9 copy-start.14
  6.5 6.6 copy-start.15
  6.6 7.4 copy-start.13
  6.6 7.3 copy-start.12
  6.6 55.8 %all-gather.7.cloned.1.call-start = ((), (), s32[]{:S(2)}) async-start(), calls=%async_computation | async-start | bytes 1081344 | tf_op jit(solution)/shard_map/all_gather | solution.py:62
  10.2 140.5 %all-gather.9.cloned.1.call-start = ((), (), s32[]{:S(2)}) async-start(), calls=%async_computation.1 | async-start | bytes 1081344 | tf_op jit(solution)/shard_map/all_gather | solution.py:10
  69.9 2.8 copy-start.6
  80.1 2.8 copy-start.6
  90.4 2.8 copy-start.6
  100.6 2.8 copy-start.6
  103.4 97.1 %all-gather.11.cloned.1.call-start = ((), (), s32[]{:S(2)}) async-start(), calls=%async_computation.2 | async-start | bytes 1081344 | tf_op jit(solution)/shard_map/all_gather | solution.py:10
  104.1 304.3 %all-gather.13.cloned.1.call-start = ((), (), s32[]{:S(2)}) async-start(), calls=%async_computation.3 | async-start | bytes 69206016 | tf_op jit(solution)/shard_map/all_gather | solution.py:10
  104.7 759.6 %all-reduce.3.cloned.1.call-start = ((), (), s32[]{:S(2)}) async-start(), calls=%async_computation.4 | async-start | bytes 524288 | tf_op jit(solution)/shard_map/psum | solution.py:119
  458.2 406.1 %copy-start.2 = (bf16[64,2048]{1,0:T(8,128)(2,1)S(1)}, bf16[64,2048]{1,0:T(8,128)(2,1)}, u32[]{:S(2)}) copy-start(bf16[64,2048]{1,0:T(8,128)(2,1)} %param.21) | copy-start | bytes 786436
  794.2 71.4 %copy-start.7 = (f32[2048]{0:T(1024)S(1)}, f32[2048]{0:T(1024)}, u32[]{:S(2)}) copy-start(f32[2048]{0:T(1024)} %param.29) | copy-start | bytes 24580
  797.5 114.6 %all-gather.15.cloned.1.call-start = ((), (), s32[]{:S(2)}) async-start(), calls=%async_computation.5 | async-start | bytes 2359296 | tf_op jit(solution)/shard_map/all_gather | solution.py:129
  864.3 3.7 copy-start.3
  868.0 3.6 copy-start.9
  868.0 3.7 copy-start.16
  871.6 42.5 %copy-start.10 = (f32[2048]{0:T(1024)S(1)}, f32[2048]{0:T(1024)}, u32[]{:S(2)}) copy-start(f32[2048]{0:T(1024)} %param.33) | copy-start | bytes 24580
  (8 other events, 9.1 us)
Sparse Core Ops, SparseCore 0:
  10.3 52.0 all-gather.6
  103.5 47.1 all-gather.8
  153.3 47.1 all-gather.10
  202.9 205.4 all-gather.12
  797.6 66.6 all-reduce.2
  871.8 40.3 all-gather.14
